TPU v7x, 32 devices: a whole 2x2x4 slice. The times are simulated.
32 devices in a mesh: group: 2 (over x), seq: 16 (over z, y, core).
Axes of the slice: x: 2, y: 2, z: 4, core: 2. Of those that a mesh axis runs over, the one named last changes fastest.
Arguments:
- query_rows: bfloat16 [16384, 2048], P(('group', 'seq')), parts along dimension 0, may hold values from -5 to 5
- key_rows: bfloat16 [16384, 2048], P(('group', 'seq')), parts along dimension 0, may hold values from -5 to 5
- value_rows: bfloat16 [16384, 2048], P(('group', 'seq')), parts along dimension 0, may hold values from -5 to 5
Outputs:
- mixed_heads: bfloat16 [16384, 2048], P(('group', 'seq')), parts along dimension 0
There are 2 independent parts, one for each index of `group`. A program takes and returns all parts, laid end to end along the dimension named above; each array names one. Nothing has to cross between parts.
All inputs are finite; a program needn't handle non-finite values.
Results may differ from a plain program's by a relative error of at most 0.0034.
Values may be sent and summed in bfloat16 or wider, within the bound.
A program may use at most 192 MiB of HBM per device.

v0:
```python
import math

import jax
import jax.numpy as jnp
from jax import lax
from jax.sharding import PartitionSpec as P

H = 16
DH = 128
WINDOW = 2048
BLOCK = 128


EPSILON = 1e-06


def entering(part, axis, combine, identity):
    place = lax.axis_index(axis)
    gathered = lax.all_gather(part, axis)
    state = jnp.zeros_like(part) + jnp.asarray(identity, part.dtype)

    def one(lap, state):
        return combine(state, lax.dynamic_index_in_dim(gathered, lap, 0, False))

    return lax.fori_loop(0, place, one, state)


def from_behind(array, axis, by):
    peers = lax.axis_size(axis)
    pairs = [(i, i + by) for i in range(peers) if 0 <= i + by < peers]
    return lax.ppermute(array, axis, pairs)


def head_norm(vectors):
    return vectors * lax.rsqrt(jnp.mean(vectors * vectors, axis=-1, keepdims=True) + EPSILON)


def add_states(earlier, later):
    return earlier + later


def linear_part(query_rows, key_rows, value_rows):
    tok_rows = query_rows.shape[0]
    block_count = tok_rows // BLOCK
    q_blocks = query_rows.reshape(block_count, BLOCK, H, DH)
    k_blocks = key_rows.reshape(block_count, BLOCK, H, DH)
    v_blocks = value_rows.reshape(block_count, BLOCK, H, DH)
    causal = jnp.arange(BLOCK)[:, None] >= jnp.arange(BLOCK)[None, :]
    block_scores = jnp.einsum(
        "bqhd,bkhd->bhqk", q_blocks, k_blocks, preferred_element_type=jnp.float32
    )
    block_scores = jnp.where(causal, block_scores, 0.0).astype(jnp.bfloat16)
    inner_term = jnp.einsum(
        "bhqk,bkhd->bqhd", block_scores, v_blocks, preferred_element_type=jnp.float32
    )
    totals = jnp.einsum("bkhd,bkhe->bhde", k_blocks, v_blocks, preferred_element_type=jnp.float32)
    earlier_local = jnp.concatenate(
        [jnp.zeros_like(totals[:1]), jnp.cumsum(totals[:-1], axis=0)], axis=0
    )
    own_total = jnp.sum(totals, axis=0)
    prefix = entering(own_total, "seq", add_states, jnp.zeros_like(own_total))
    starts = prefix[None] + earlier_local
    cross_term = jnp.einsum(
        "bqhd,bhde->bqhe", q_blocks.astype(jnp.float32), starts, precision=lax.Precision.HIGHEST
    )
    return (cross_term + inner_term).reshape(tok_rows, H, DH)


def window_part(query_rows, key_rows, value_rows):
    tok_rows = query_rows.shape[0]
    shards_back = WINDOW // tok_rows
    earlier = [
        from_behind((key_rows, value_rows), "seq", distance)
        for distance in range(shards_back, 0, -1)
    ]
    all_keys = jnp.concatenate([shard_pair[0] for shard_pair in earlier] + [key_rows], axis=0)
    all_values = jnp.concatenate([shard_pair[1] for shard_pair in earlier] + [value_rows], axis=0)
    key_span = all_keys.shape[0]
    heads_q = query_rows.reshape(tok_rows, H, DH).transpose(1, 0, 2)
    heads_k = all_keys.reshape(key_span, H, DH).transpose(1, 0, 2)
    heads_v = all_values.reshape(key_span, H, DH).transpose(1, 0, 2)
    query_span = min(512, tok_rows)
    first_position = lax.axis_index("seq") * tok_rows
    score_scale = 1.0 / math.sqrt(DH)

    def one_head(pieces):
        head_q, head_k, head_v = pieces
        query_pos = first_position + 0 + jnp.arange(query_span, dtype=jnp.int32)
        key_pos = first_position + 0 - WINDOW + jnp.arange(WINDOW + query_span, dtype=jnp.int32)
        allowed = (
            (key_pos[None, :] <= query_pos[:, None])
            & (key_pos[None, :] > query_pos[:, None] - WINDOW)
            & (key_pos[None, :] >= 0)
        )
        scores = (
            jnp.einsum("qd,kd->qk", head_q, head_k, preferred_element_type=jnp.float32)
            * score_scale
        )
        scores = jnp.where(allowed, scores, -1e30)
        row_peak = jnp.max(scores, axis=-1, keepdims=True)
        weights = jnp.exp(scores - row_peak)
        weights = weights / jnp.sum(weights, axis=-1, keepdims=True)
        weights = weights.astype(jnp.bfloat16)
        outputs = [jnp.einsum("qk,kd->qd", weights, head_v, preferred_element_type=jnp.float32)]
        return jnp.concatenate(outputs, axis=0)

    window = lax.map(one_head, (heads_q, heads_k, heads_v))
    return window.transpose(1, 0, 2)


def per_device(query_rows, key_rows, value_rows):
    tok_rows = query_rows.shape[0]
    linear = linear_part(query_rows, key_rows, value_rows)
    window = window_part(query_rows, key_rows, value_rows)
    mixed_out = head_norm(linear) + head_norm(window)
    return mixed_out.reshape(tok_rows, H * DH).astype(jnp.bfloat16)


def solution(mesh):
    return jax.shard_map(
        per_device,
        mesh=mesh,
        in_specs=(P(("group", "seq"), None), P(("group", "seq"), None), P(("group", "seq"), None)),
        out_specs=P(("group", "seq"), None),
        check_vma=False,
    )
```

profile of v0, /device:TPU:24, one launch (start us, length us, event | category | flops | bytes accessed | tf_op | source)
XLA Modules:
  0.0 719.5 jit_solution(6297317294097977793)
XLA Ops:
  28.0 67.0 %collective-permute-done.4 = bf16[512,2048]{0,1:T(8,128)(2,1)} collective-permute-done((bf16[512,2048]{0,1:T(8,128)(2,1)}, bf16[512,2048]{0,1:T(8,128)(2,1)}, u32[]{:S(2)}, u32[]{:S(2)}) %collective-permute-start.4) | collective-permute-done | bytes 2097184 | tf_op jit(solution)/shard_map/ppermute | solution.py:31
  96.9 83.1 %collective-permute-done.5 = bf16[512,2048]{0,1:T(8,128)(2,1)} collective-permute-done((bf16[512,2048]{0,1:T(8,128)(2,1)}, bf16[512,2048]{0,1:T(8,128)(2,1)}, u32[]{:S(2)}, u32[]{:S(2)}) %collective-permute-start.5) | collective-permute-done | bytes 2097184 | tf_op jit(solution)/shard_map/ppermute | solution.py:31
  190.9 62.3 %collective-permute-done.6 = bf16[512,2048]{0,1:T(8,128)(2,1)} collective-permute-done((bf16[512,2048]{0,1:T(8,128)(2,1)}, bf16[512,2048]{0,1:T(8,128)(2,1)}, u32[]{:S(2)}, u32[]{:S(2)}) %collective-permute-start.6) | collective-permute-done | bytes 2097184 | tf_op jit(solution)/shard_map/ppermute | solution.py:31
  260.5 35.4 %collective-permute-done.7 = bf16[512,2048]{0,1:T(8,128)(2,1)} collective-permute-done((bf16[512,2048]{0,1:T(8,128)(2,1)}, bf16[512,2048]{0,1:T(8,128)(2,1)}, u32[]{:S(2)}, u32[]{:S(2)}) %collective-permute-start.7) | collective-permute-done | bytes 2097184 | tf_op jit(solution)/shard_map/ppermute | solution.py:31
  303.9 84.2 %collective-permute-done.2 = bf16[512,2048]{0,1:T(8,128)(2,1)} collective-permute-done((bf16[512,2048]{0,1:T(8,128)(2,1)}, bf16[512,2048]{0,1:T(8,128)(2,1)}, u32[]{:S(2)}, u32[]{:S(2)}) %collective-permute-start.2) | collective-permute-done | bytes 2097184 | tf_op jit(solution)/shard_map/ppermute | solution.py:31
  389.8 42.0 %collective-permute-done.3 = bf16[512,2048]{0,1:T(8,128)(2,1)S(1)} collective-permute-done((bf16[512,2048]{0,1:T(8,128)(2,1)}, bf16[512,2048]{0,1:T(8,128)(2,1)S(1)}, u32[]{:S(2)}, u32[]{:S(2)}) %collective-permute-start.3) | collective-permute-done | bytes 2097184 | tf_op jit(solution)/shard_map/ppermute | solution.py:31
  436.1 225.3 %while.24 = (s32[]{:T(128)}, f32[16,512,128]{2,0,1:T(8,128)}, s32[]{:T(128)}, s32[]{:T(128)}, bf16[16,512,128]{1,2,0:T(8,128)(2,1)}, /*index=5*/bf16[16,2560,128...) while((s32[]{:T(128)}, f32[16,512,128]{2,0,1:T(8,128)}, s32[]{:T(128)}, s32[]{:T(128)}, ...), condition=%wide.region_8.9_spmd, body=%wide.region_5.8_spmd.sunk | while | flops 686824960 | bytes 18002540 | solution.py:107
  442.1 8.1 %dynamic_update_slice.9 = f32[16,512,128]{2,0,1:T(8,128)} dynamic-update-slice(f32[16,512,128]{2,0,1:T(8,128)} %get-tuple-element.285, f32[1,512,128]{2,0,1:T(1,128)S(1)} %bitcast.82, s32[]{:T(128)} %get-tuple-element.284, s32[]{:T(128)} %constant.80.clone.1..sunk.1, s32[]{:T(128)} %constant.80.clone.1..sunk.1) | dynamic-update-slice | bytes 524292 | tf_op jit(solution)/shard_map/while/body/jit(dynamic_update_index_in_dim)/dynamic_update_slice | solution.py:107
  456.1 8.1 %dynamic_update_slice.9 = f32[16,512,128]{2,0,1:T(8,128)} dynamic-update-slice(f32[16,512,128]{2,0,1:T(8,128)} %get-tuple-element.285, f32[1,512,128]{2,0,1:T(1,128)S(1)} %bitcast.82, s32[]{:T(128)} %get-tuple-element.284, s32[]{:T(128)} %constant.80.clone.1..sunk.1, s32[]{:T(128)} %constant.80.clone.1..sunk.1) | dynamic-update-slice | bytes 524292 | tf_op jit(solution)/shard_map/while/body/jit(dynamic_update_index_in_dim)/dynamic_update_slice | solution.py:107
  470.2 8.1 %dynamic_update_slice.9 = f32[16,512,128]{2,0,1:T(8,128)} dynamic-update-slice(f32[16,512,128]{2,0,1:T(8,128)} %get-tuple-element.285, f32[1,512,128]{2,0,1:T(1,128)S(1)} %bitcast.82, s32[]{:T(128)} %get-tuple-element.284, s32[]{:T(128)} %constant.80.clone.1..sunk.1, s32[]{:T(128)} %constant.80.clone.1..sunk.1) | dynamic-update-slice | bytes 524292 | tf_op jit(solution)/shard_map/while/body/jit(dynamic_update_index_in_dim)/dynamic_update_slice | solution.py:107
  484.3 8.1 %dynamic_update_slice.9 = f32[16,512,128]{2,0,1:T(8,128)} dynamic-update-slice(f32[16,512,128]{2,0,1:T(8,128)} %get-tuple-element.285, f32[1,512,128]{2,0,1:T(1,128)S(1)} %bitcast.82, s32[]{:T(128)} %get-tuple-element.284, s32[]{:T(128)} %constant.80.clone.1..sunk.1, s32[]{:T(128)} %constant.80.clone.1..sunk.1) | dynamic-update-slice | bytes 524292 | tf_op jit(solution)/shard_map/while/body/jit(dynamic_update_index_in_dim)/dynamic_update_slice | solution.py:107
  498.4 8.1 %dynamic_update_slice.9 = f32[16,512,128]{2,0,1:T(8,128)} dynamic-update-slice(f32[16,512,128]{2,0,1:T(8,128)} %get-tuple-element.285, f32[1,512,128]{2,0,1:T(1,128)S(1)} %bitcast.82, s32[]{:T(128)} %get-tuple-element.284, s32[]{:T(128)} %constant.80.clone.1..sunk.1, s32[]{:T(128)} %constant.80.clone.1..sunk.1) | dynamic-update-slice | bytes 524292 | tf_op jit(solution)/shard_map/while/body/jit(dynamic_update_index_in_dim)/dynamic_update_slice | solution.py:107
  512.5 8.1 %dynamic_update_slice.9 = f32[16,512,128]{2,0,1:T(8,128)} dynamic-update-slice(f32[16,512,128]{2,0,1:T(8,128)} %get-tuple-element.285, f32[1,512,128]{2,0,1:T(1,128)S(1)} %bitcast.82, s32[]{:T(128)} %get-tuple-element.284, s32[]{:T(128)} %constant.80.clone.1..sunk.1, s32[]{:T(128)} %constant.80.clone.1..sunk.1) | dynamic-update-slice | bytes 524292 | tf_op jit(solution)/shard_map/while/body/jit(dynamic_update_index_in_dim)/dynamic_update_slice | solution.py:107
  526.6 8.1 %dynamic_update_slice.9 = f32[16,512,128]{2,0,1:T(8,128)} dynamic-update-slice(f32[16,512,128]{2,0,1:T(8,128)} %get-tuple-element.285, f32[1,512,128]{2,0,1:T(1,128)S(1)} %bitcast.82, s32[]{:T(128)} %get-tuple-element.284, s32[]{:T(128)} %constant.80.clone.1..sunk.1, s32[]{:T(128)} %constant.80.clone.1..sunk.1) | dynamic-update-slice | bytes 524292 | tf_op jit(solution)/shard_map/while/body/jit(dynamic_update_index_in_dim)/dynamic_update_slice | solution.py:107
  540.6 8.1 %dynamic_update_slice.9 = f32[16,512,128]{2,0,1:T(8,128)} dynamic-update-slice(f32[16,512,128]{2,0,1:T(8,128)} %get-tuple-element.285, f32[1,512,128]{2,0,1:T(1,128)S(1)} %bitcast.82, s32[]{:T(128)} %get-tuple-element.284, s32[]{:T(128)} %constant.80.clone.1..sunk.1, s32[]{:T(128)} %constant.80.clone.1..sunk.1) | dynamic-update-slice | bytes 524292 | tf_op jit(solution)/shard_map/while/body/jit(dynamic_update_index_in_dim)/dynamic_update_slice | solution.py:107
  554.7 8.1 %dynamic_update_slice.9 = f32[16,512,128]{2,0,1:T(8,128)} dynamic-update-slice(f32[16,512,128]{2,0,1:T(8,128)} %get-tuple-element.285, f32[1,512,128]{2,0,1:T(1,128)S(1)} %bitcast.82, s32[]{:T(128)} %get-tuple-element.284, s32[]{:T(128)} %constant.80.clone.1..sunk.1, s32[]{:T(128)} %constant.80.clone.1..sunk.1) | dynamic-update-slice | bytes 524292 | tf_op jit(solution)/shard_map/while/body/jit(dynamic_update_index_in_dim)/dynamic_update_slice | solution.py:107
  568.8 8.1 %dynamic_update_slice.9 = f32[16,512,128]{2,0,1:T(8,128)} dynamic-update-slice(f32[16,512,128]{2,0,1:T(8,128)} %get-tuple-element.285, f32[1,512,128]{2,0,1:T(1,128)S(1)} %bitcast.82, s32[]{:T(128)} %get-tuple-element.284, s32[]{:T(128)} %constant.80.clone.1..sunk.1, s32[]{:T(128)} %constant.80.clone.1..sunk.1) | dynamic-update-slice | bytes 524292 | tf_op jit(solution)/shard_map/while/body/jit(dynamic_update_index_in_dim)/dynamic_update_slice | solution.py:107
  582.9 8.1 %dynamic_update_slice.9 = f32[16,512,128]{2,0,1:T(8,128)} dynamic-update-slice(f32[16,512,128]{2,0,1:T(8,128)} %get-tuple-element.285, f32[1,512,128]{2,0,1:T(1,128)S(1)} %bitcast.82, s32[]{:T(128)} %get-tuple-element.284, s32[]{:T(128)} %constant.80.clone.1..sunk.1, s32[]{:T(128)} %constant.80.clone.1..sunk.1) | dynamic-update-slice | bytes 524292 | tf_op jit(solution)/shard_map/while/body/jit(dynamic_update_index_in_dim)/dynamic_update_slice | solution.py:107
  597.0 8.1 %dynamic_update_slice.9 = f32[16,512,128]{2,0,1:T(8,128)} dynamic-update-slice(f32[16,512,128]{2,0,1:T(8,128)} %get-tuple-element.285, f32[1,512,128]{2,0,1:T(1,128)S(1)} %bitcast.82, s32[]{:T(128)} %get-tuple-element.284, s32[]{:T(128)} %constant.80.clone.1..sunk.1, s32[]{:T(128)} %constant.80.clone.1..sunk.1) | dynamic-update-slice | bytes 524292 | tf_op jit(solution)/shard_map/while/body/jit(dynamic_update_index_in_dim)/dynamic_update_slice | solution.py:107
  611.0 8.1 %dynamic_update_slice.9 = f32[16,512,128]{2,0,1:T(8,128)} dynamic-update-slice(f32[16,512,128]{2,0,1:T(8,128)} %get-tuple-element.285, f32[1,512,128]{2,0,1:T(1,128)S(1)} %bitcast.82, s32[]{:T(128)} %get-tuple-element.284, s32[]{:T(128)} %constant.80.clone.1..sunk.1, s32[]{:T(128)} %constant.80.clone.1..sunk.1) | dynamic-update-slice | bytes 524292 | tf_op jit(solution)/shard_map/while/body/jit(dynamic_update_index_in_dim)/dynamic_update_slice | solution.py:107
  625.1 8.1 %dynamic_update_slice.9 = f32[16,512,128]{2,0,1:T(8,128)} dynamic-update-slice(f32[16,512,128]{2,0,1:T(8,128)} %get-tuple-element.285, f32[1,512,128]{2,0,1:T(1,128)S(1)} %bitcast.82, s32[]{:T(128)} %get-tuple-element.284, s32[]{:T(128)} %constant.80.clone.1..sunk.1, s32[]{:T(128)} %constant.80.clone.1..sunk.1) | dynamic-update-slice | bytes 524292 | tf_op jit(solution)/shard_map/while/body/jit(dynamic_update_index_in_dim)/dynamic_update_slice | solution.py:107
  639.2 8.1 %dynamic_update_slice.9 = f32[16,512,128]{2,0,1:T(8,128)} dynamic-update-slice(f32[16,512,128]{2,0,1:T(8,128)} %get-tuple-element.285, f32[1,512,128]{2,0,1:T(1,128)S(1)} %bitcast.82, s32[]{:T(128)} %get-tuple-element.284, s32[]{:T(128)} %constant.80.clone.1..sunk.1, s32[]{:T(128)} %constant.80.clone.1..sunk.1) | dynamic-update-slice | bytes 524292 | tf_op jit(solution)/shard_map/while/body/jit(dynamic_update_index_in_dim)/dynamic_update_slice | solution.py:107
  653.3 8.1 %dynamic_update_slice.9 = f32[16,512,128]{2,0,1:T(8,128)} dynamic-update-slice(f32[16,512,128]{2,0,1:T(8,128)} %get-tuple-element.285, f32[1,512,128]{2,0,1:T(1,128)S(1)} %bitcast.82, s32[]{:T(128)} %get-tuple-element.284, s32[]{:T(128)} %constant.80.clone.1..sunk.1, s32[]{:T(128)} %constant.80.clone.1..sunk.1) | dynamic-update-slice | bytes 524292 | tf_op jit(solution)/shard_map/while/body/jit(dynamic_update_index_in_dim)/dynamic_update_slice | solution.py:107
  665.1 18.4 %while.23 = (s32[]{:T(128)}, f32[16,128,128]{2,1,0:T(8,128)S(1)}, s32[]{:T(128)}, f32[16,16,128,128]{3,2,1,0:T(8,128)}, s32[]{:T(128)}, /*index=5*/s32[]{:T(128)}, s32[]{:T(128)}) while((s32[]{:T(128)}, f32[16,128,128]{2,1,0:T(8,128)S(1)}, s32[]{:T(128)}, f32[16,16,128,128]{3,2,1,0:T(8,128)}, s32[]{:T(128)}, /*index=5*/s32[]{:T(128)}, ...), condition=%wide.region_2.3_spmd, body=%wide.region_1.2_spmd.sunk | while | flops 262149 | bytes 3145843 | solution.py:25
  (171 shorter events, 201.8 us)
Async XLA Ops:
  6.5 12.1 %copy-start.2 = (bf16[512,2048]{1,0:T(8,128)(2,1)S(1)}, bf16[512,2048]{1,0:T(8,128)(2,1)}, u32[]{:S(2)}) copy-start(bf16[512,2048]{1,0:T(8,128)(2,1)} %param.8) | copy-start | bytes 6291460
  6.5 658.4 %all-gather.3.cloned.1.call-start = ((), (), s32[]{:S(2)}) async-start(), calls=%async_computation | async-start | bytes 17825792 | tf_op jit(solution)/shard_map/all_gather | solution.py:19
  10.6 84.4 %collective-permute-start.4 = (bf16[512,2048]{0,1:T(8,128)(2,1)}, bf16[512,2048]{0,1:T(8,128)(2,1)}, u32[]{:S(2)}, u32[]{:S(2)}) collective-permute-start(bf16[512,2048]{0,1:T(8,128)(2,1)} %copy.115), channel_id=1, source_target_pairs={{0,4},{1,5},{2,6},{3,7},{4,8},{5,9},{6,10},{7,11},{8,12},{9,13},{1... | collective-permute-start | bytes 6291464 | tf_op jit(solution)/shard_map/ppermute | solution.py:31
  11.9 168.2 %collective-permute-start.5 = (bf16[512,2048]{0,1:T(8,128)(2,1)}, bf16[512,2048]{0,1:T(8,128)(2,1)}, u32[]{:S(2)}, u32[]{:S(2)}) collective-permute-start(bf16[512,2048]{0,1:T(8,128)(2,1)} %copy.115), channel_id=1, source_target_pairs={{0,3},{1,4},{2,5},{3,6},{4,7},{5,8},{6,9},{7,10},{8,11},{9,12},{10... | collective-permute-start | bytes 6291464 | tf_op jit(solution)/shard_map/ppermute | solution.py:31
  14.8 238.5 %collective-permute-start.6 = (bf16[512,2048]{0,1:T(8,128)(2,1)}, bf16[512,2048]{0,1:T(8,128)(2,1)}, u32[]{:S(2)}, u32[]{:S(2)}) collective-permute-start(bf16[512,2048]{0,1:T(8,128)(2,1)} %copy.115), channel_id=1, source_target_pairs={{0,2},{1,3},{2,4},{3,5},{4,6},{5,7},{6,8},{7,9},{8,10},{9,11},{10,... | collective-permute-start | bytes 6291464 | tf_op jit(solution)/shard_map/ppermute | solution.py:31
  16.7 279.2 %collective-permute-start.7 = (bf16[512,2048]{0,1:T(8,128)(2,1)}, bf16[512,2048]{0,1:T(8,128)(2,1)}, u32[]{:S(2)}, u32[]{:S(2)}) collective-permute-start(bf16[512,2048]{0,1:T(8,128)(2,1)} %copy.115), channel_id=1, source_target_pairs={{0,1},{1,2},{2,3},{3,4},{4,5},{5,6},{6,7},{7,8},{8,9},{9,10},{10,1... | collective-permute-start | bytes 6291464 | tf_op jit(solution)/shard_map/ppermute | solution.py:31
  21.1 2.0 copy-start.3
  21.1 276.7 %collective-permute-start = (bf16[512,2048]{0,1:T(8,128)(2,1)}, bf16[512,2048]{0,1:T(8,128)(2,1)}, u32[]{:S(2)}, u32[]{:S(2)}) collective-permute-start(bf16[512,2048]{0,1:T(8,128)(2,1)} %copy.110), channel_id=1, source_target_pairs={{0,4},{1,5},{2,6},{3,7},{4,8},{5,9},{6,10},{7,11},{8,12},{9,13},{1... | collective-permute-start | bytes 6291464 | tf_op jit(solution)/shard_map/ppermute | solution.py:31
  23.2 4.8 copy-start
  23.8 4.1 copy-start.1
  28.0 158.2 %copy-start.4 = (bf16[512,2048]{1,0:T(8,128)(2,1)S(1)}, bf16[512,2048]{1,0:T(8,128)(2,1)}, u32[]{:S(2)}) copy-start(bf16[512,2048]{1,0:T(8,128)(2,1)} %param.7) | copy-start | bytes 6291460
  95.0 206.1 %collective-permute-start.1 = (bf16[512,2048]{0,1:T(8,128)(2,1)}, bf16[512,2048]{0,1:T(8,128)(2,1)}, u32[]{:S(2)}, u32[]{:S(2)}) collective-permute-start(bf16[512,2048]{0,1:T(8,128)(2,1)} %copy.110), channel_id=1, source_target_pairs={{0,3},{1,4},{2,5},{3,6},{4,7},{5,8},{6,9},{7,10},{8,11},{9,12},{10... | collective-permute-start | bytes 6291464 | tf_op jit(solution)/shard_map/ppermute | solution.py:31
  180.0 208.0 %collective-permute-start.2 = (bf16[512,2048]{0,1:T(8,128)(2,1)}, bf16[512,2048]{0,1:T(8,128)(2,1)}, u32[]{:S(2)}, u32[]{:S(2)}) collective-permute-start(bf16[512,2048]{0,1:T(8,128)(2,1)} %copy.110), channel_id=1, source_target_pairs={{0,2},{1,3},{2,4},{3,5},{4,6},{5,7},{6,8},{7,9},{8,10},{9,11},{10,... | collective-permute-start | bytes 6291464 | tf_op jit(solution)/shard_map/ppermute | solution.py:31
  253.3 178.5 %collective-permute-start.3 = (bf16[512,2048]{0,1:T(8,128)(2,1)}, bf16[512,2048]{0,1:T(8,128)(2,1)S(1)}, u32[]{:S(2)}, u32[]{:S(2)}) collective-permute-start(bf16[512,2048]{0,1:T(8,128)(2,1)} %copy.110), channel_id=1, source_target_pairs={{0,1},{1,2},{2,3},{3,4},{4,5},{5,6},{6,7},{7,8},{8,9},{9,10},{10,1... | collective-permute-start | bytes 6291464 | tf_op jit(solution)/shard_map/ppermute | solution.py:31
  258.6 39.0 %copy-start.6 = (bf16[512,2048]{0,1:T(8,128)(2,1)S(1)}, bf16[512,2048]{0,1:T(8,128)(2,1)}, u32[]{:S(2)}) copy-start(bf16[512,2048]{0,1:T(8,128)(2,1)} %copy.115) | copy-start | bytes 6291460
  297.8 134.3 %copy-start.8 = (bf16[2560,2048]{0,1:T(8,128)(2,1)}, bf16[2560,2048]{0,1:T(8,128)(2,1)S(1)}, u32[]{:S(2)}) copy-start(bf16[2560,2048]{0,1:T(8,128)(2,1)S(1)} %constant_dynamic-update-slice_fusion.5) | copy-start | bytes 31457284
  303.9 128.1 %copy-start.5 = (bf16[512,2048]{0,1:T(8,128)(2,1)S(1)}, bf16[512,2048]{0,1:T(8,128)(2,1)}, u32[]{:S(2)}) copy-start(bf16[512,2048]{0,1:T(8,128)(2,1)} %copy.110) | copy-start | bytes 6291460
  432.1 4.0 copy-start.7
Sparse Core Ops, SparseCore 0:
  28.1 190.0 all-gather.2
where the time goes:
time: 724 us; the launch traced here: 720 us
  waiting for transfers between devices  374 us (52%)
  local copies, waits for them, and re-layouts  170 us (23%)
  matrix products  101 us (14%)
  other arithmetic  45.2 us (6%)
  starting transfers between devices  15.4 us (2%)
  between operations  13.7 us (2%)
    ppermute x8, waiting for transfers between devices, from_behind(): return lax.ppermute(array, axis, pairs)  374 us
    dynamic_update_slice x16, local copies, waits for them, and re-layouts, window_part(): window = lax.map(one_head, (heads_q, heads_k, heads_v))  129 us
    dot_general x16, matrix products, one_head(): jnp.einsum('qd,kd->qk', head_q, head_k, preferred_element_type=jnp.float32)  48.8 us
    unnamed x33, local copies, waits for them, and re-layouts  33.3 us
    dot_general x16, matrix products, one_head(): jnp.einsum('qk,kd->qd', weights, head_v, preferred_element_type=jnp.float32)  33.2 us
    add x12, other arithmetic, add_states(): return earlier + later  17.9 us
    ppermute x8, starting transfers between devices, from_behind(): return lax.ppermute(array, axis, pairs)  15.4 us
  transfers between devices with their start and end apart: 9, of which 6 were waited for; matrix products, arithmetic and copies ran while one was open for 36% of the time, Pallas kernels for 0%

commit v1 on v0

v1 whole, which is shorter than its diff:
```python
import functools
import math

import jax
import jax.numpy as jnp
from jax import lax
from jax.experimental import pallas as pl
from jax.experimental.pallas import tpu as pltpu
from jax.sharding import PartitionSpec as P

H = 16
DH = 128
WINDOW = 2048
TILE = 256
EPSILON = 1e-06
EXP_SCALE = math.log2(math.e) / math.sqrt(DH)
NEG = -1e30
F32 = jnp.float32
BF16 = jnp.bfloat16
MESH = pl.DeviceIdType.MESH


def dot_nt(a, b):
    return lax.dot_general(a, b, (((1,), (1,)), ((), ())), preferred_element_type=F32)


def dot_tn(a, b):
    return lax.dot_general(a, b, (((0,), (0,)), ((), ())), preferred_element_type=F32)


def dot_nn(a, b):
    return jnp.dot(a, b, preferred_element_type=F32)


def times_state(q, state):
    high = state.astype(BF16)
    low = (state - high.astype(F32)).astype(BF16)
    both = dot_nn(q, jnp.concatenate([high, low], axis=1))
    return both[:, :DH] + both[:, DH:]


def head_norm(x):
    return x * lax.rsqrt(jnp.mean(x * x, axis=-1, keepdims=True) + EPSILON)


def kernel(
    layer, layers, rows,
    q_hbm, k_hbm, v_hbm, out_hbm,
    qb, kb, vb, kh, vh, ob, o_acc, m_acc, l_acc, lin_acc, total, state_in, state_out,
    own_sem, a_send, a_recv, z_send, z_recv, s_send, s_recv, o_own, o_send, o_recv,
):
    me = lax.axis_index("seq")
    place = lax.rem(me, layer)
    level = me // layer
    base = level * layer
    heads = H // layer
    span = layer * rows
    tiles = span // TILE
    has_before = level > 0
    has_after = level < layers - 1

    def peer(d):
        return base + lax.rem(place + d, layer)

    barrier = pltpu.get_barrier_semaphore()
    for d in range(1, layer):
        pl.semaphore_signal(barrier, inc=1, device_id={"seq": peer(d)}, device_id_type=MESH)

    @pl.when(has_before)
    def _():
        pl.semaphore_signal(barrier, inc=1, device_id={"seq": me - layer}, device_id_type=MESH)

    @pl.when(has_after)
    def _():
        pl.semaphore_signal(barrier, inc=1, device_id={"seq": me + layer}, device_id_type=MESH)

    ends = has_before.astype(jnp.int32) + has_after.astype(jnp.int32)
    pl.semaphore_wait(barrier, layer - 1 + ends)

    sources = (k_hbm, v_hbm, q_hbm)
    targets = (kb, vb, qb)

    def columns(owner, c):
        return pl.ds(pl.multiple_of((owner * heads + c) * DH, DH), DH)

    my_rows = pl.ds(pl.multiple_of(place * rows, rows), rows)

    def own_copy(c, t):
        return pltpu.make_async_copy(
            sources[t].at[:, columns(place, c)], targets[t].at[c, my_rows, :], own_sem.at[c, t]
        )

    def peer_copy(c, d, t):
        return pltpu.make_async_remote_copy(
            src_ref=sources[t].at[:, columns(lax.rem(place + d, layer), c)],
            dst_ref=targets[t].at[c, my_rows, :],
            send_sem=a_send.at[c, d - 1, t],
            recv_sem=a_recv.at[c, d - 1, t],
            device_id={"seq": peer(d)},
            device_id_type=MESH,
        )

    def next_copy(c, t):
        return pltpu.make_async_remote_copy(
            src_ref=(kb, vb)[t].at[c],
            dst_ref=(kh, vh)[t].at[c],
            send_sem=z_send.at[c, t],
            recv_sem=z_recv.at[c, t],
            device_id={"seq": me + layer},
            device_id_type=MESH,
        )

    def state_copy(c):
        return pltpu.make_async_remote_copy(
            src_ref=state_out.at[c],
            dst_ref=state_in.at[c],
            send_sem=s_send.at[c],
            recv_sem=s_recv.at[c],
            device_id={"seq": me + layer},
            device_id_type=MESH,
        )

    def out_copy(c, d):
        to_rows = pl.ds(pl.multiple_of(lax.rem(place + d, layer) * rows, rows), rows)
        return pltpu.make_async_remote_copy(
            src_ref=ob.at[c, to_rows, :],
            dst_ref=out_hbm.at[:, columns(place, c)],
            send_sem=o_send.at[c, d - 1],
            recv_sem=o_recv.at[c, d - 1],
            device_id={"seq": peer(d)},
            device_id_type=MESH,
        )

    def out_own(c):
        return pltpu.make_async_copy(
            ob.at[c, my_rows, :], out_hbm.at[:, columns(place, c)], o_own.at[c]
        )

    def start_chunk(c):
        for t in range(3):
            for d in range(layer - 1, 0, -1):
                peer_copy(c, d, t).start()
            own_copy(c, t).start()

    def wait_tensor(c, t):
        own_copy(c, t).wait()
        for d in range(1, layer):
            peer_copy(c, d, t).wait_recv()

    row_id = lax.broadcasted_iota(jnp.int32, (TILE, TILE), 0)
    col_id = lax.broadcasted_iota(jnp.int32, (TILE, TILE), 1)

    def part_softmax(q, k_full, v_full, s_diag, v_diag):
        peak = jnp.max(s_diag, axis=-1, keepdims=True)
        if k_full is not None:
            s_full = dot_nt(q, k_full)
            peak = jnp.maximum(peak, jnp.max(s_full, axis=-1, keepdims=True))
        p_diag = jnp.exp2((s_diag - peak) * EXP_SCALE)
        mass = jnp.sum(p_diag, axis=-1, keepdims=True)
        acc = dot_nn(p_diag.astype(BF16), v_diag)
        if k_full is not None:
            p_full = jnp.exp2((s_full - peak) * EXP_SCALE)
            mass = mass + jnp.sum(p_full, axis=-1, keepdims=True)
            acc = acc + dot_nn(p_full.astype(BF16), v_full)
        return peak, mass, acc

    def local_part(c, slot):
        causal = row_id >= col_id
        state = jnp.zeros((DH, DH), F32)
        for i in range(tiles):
            here = slice(i * TILE, (i + 1) * TILE)
            q, k, v = qb[c, here, :], kb[c, here, :], vb[c, here, :]
            scores = dot_nt(q, k)
            lin = dot_nn(jnp.where(causal, scores, 0.0).astype(BF16), v)
            if i > 0:
                lin = lin + times_state(q, state)
            lin_acc[slot, here, :] = lin
            state = state + dot_tn(k, v)
            k_full = kb[c, : i * TILE, :] if i > 0 else None
            v_full = vb[c, : i * TILE, :] if i > 0 else None
            peak, mass, acc = part_softmax(q, k_full, v_full, jnp.where(causal, scores, NEG), v)
            o_acc[slot, here, :] = acc
            m_acc[slot, here, :] = jnp.broadcast_to(peak, (TILE, DH))
            l_acc[slot, here, :] = jnp.broadcast_to(mass, (TILE, DH))
        total[c] = state

    def halo_part(c, slot):
        inside = col_id > row_id
        state = state_in[c]
        for i in range(tiles):
            here = slice(i * TILE, (i + 1) * TILE)
            q, k, v = qb[c, here, :], kh[c, here, :], vh[c, here, :]
            scores = jnp.where(inside, dot_nt(q, k), NEG)
            lin_acc[slot, here, :] += times_state(q, state)
            k_full = kh[c, (i + 1) * TILE :, :] if i < tiles - 1 else None
            v_full = vh[c, (i + 1) * TILE :, :] if i < tiles - 1 else None
            peak, mass, acc = part_softmax(q, k_full, v_full, scores, v)
            before = m_acc[slot, here, :]
            both = jnp.maximum(before, peak)
            keep = jnp.exp2((before - both) * EXP_SCALE)
            take = jnp.exp2((peak - both) * EXP_SCALE)
            o_acc[slot, here, :] = o_acc[slot, here, :] * keep + acc * take
            l_acc[slot, here, :] = l_acc[slot, here, :] * keep + mass * take

    start_chunk(0)
    if heads > 1:
        start_chunk(1)

    def step(c, _):
        @pl.when(c < heads)
        def _():
            wait_tensor(c, 0)
            wait_tensor(c, 1)

            @pl.when(has_after)
            def _():
                next_copy(c, 0).start()
                next_copy(c, 1).start()

            @pl.when(c + 2 < heads)
            def _():
                start_chunk(c + 2)

            wait_tensor(c, 2)
            local_part(c, lax.rem(c, 2))

        @pl.when(c > 0)
        def _():
            h = c - 1
            slot = lax.rem(h, 2)

            @pl.when(has_before)
            def _():
                state_copy(h).wait_recv()

            @pl.when(has_after)
            def _():
                @pl.when(has_before)
                def _():
                    state_out[h] = state_in[h] + total[h]

                @pl.when(level == 0)
                def _():
                    state_out[h] = total[h]

                state_copy(h).start()

            @pl.when(has_before)
            def _():
                next_copy(h, 0).wait_recv()
                next_copy(h, 1).wait_recv()
                halo_part(h, slot)

            def finish(i, _):
                here = pl.ds(pl.multiple_of(i * TILE, TILE), TILE)
                win = o_acc[slot, here, :] / l_acc[slot, here, :]
                ob[h, here, :] = (head_norm(lin_acc[slot, here, :]) + head_norm(win)).astype(BF16)
                return 0

            lax.fori_loop(0, tiles, finish, 0)
            for d in range(1, layer):
                out_copy(h, d).start()
            out_own(h).start()

        return 0

    lax.fori_loop(0, heads + 1, step, 0)

    def drain(c, _):
        for d in range(1, layer):
            for t in range(3):
                peer_copy(c, d, t).wait_send()
            out_copy(c, d).wait_send()
            out_copy(c, d).wait_recv()
        out_own(c).wait()

        @pl.when(has_after)
        def _():
            next_copy(c, 0).wait_send()
            next_copy(c, 1).wait_send()
            state_copy(c).wait_send()

        return 0

    lax.fori_loop(0, heads, drain, 0)


def per_device(query_rows, key_rows, value_rows):
    rows = query_rows.shape[0]
    layer = WINDOW // rows
    layers = lax.axis_size("seq") // layer
    heads = H // layer
    span = layer * rows
    dma = pltpu.SemaphoreType.DMA
    return pl.pallas_call(
        functools.partial(kernel, layer, layers, rows),
        out_shape=jax.ShapeDtypeStruct(query_rows.shape, BF16),
        in_specs=[pl.BlockSpec(memory_space=pl.ANY)] * 3,
        out_specs=pl.BlockSpec(memory_space=pl.ANY),
        scratch_shapes=[pltpu.VMEM((heads, span, DH), BF16)] * 6
        + [pltpu.VMEM((2, span, DH), F32)] * 4
        + [pltpu.VMEM((heads, DH, DH), F32)] * 3
        + [
            dma((heads, 3)),
            dma((heads, layer - 1, 3)),
            dma((heads, layer - 1, 3)),
            dma((heads, 2)),
            dma((heads, 2)),
            dma((heads,)),
            dma((heads,)),
            dma((heads,)),
            dma((heads, layer - 1)),
            dma((heads, layer - 1)),
        ],
        compiler_params=pltpu.CompilerParams(
            collective_id=0, has_side_effects=True, vmem_limit_bytes=56 * 2**20
        ),
    )(query_rows, key_rows, value_rows)


def solution(mesh):
    spec = P(("group", "seq"), None)
    return jax.shard_map(
        per_device, mesh=mesh, in_specs=(spec, spec, spec), out_specs=spec, check_vma=False
    )
```

time: 724 us -> 138 us (0.19)
  waiting for transfers between devices: 374 us -> 0 us
  local copies, waits for them, and re-layouts: 170 us -> 3.16 us
  Pallas kernels: 0 us -> 133 us
  matrix products: 101 us -> 0 us
  other arithmetic: 45.2 us -> 0 us
  starting transfers between devices: 15.4 us -> 0 us
  between operations: 13.7 us -> 0.01 us
    ppermute x8 -> x0, waiting for transfers between devices: 374 us -> none  [from_behind(): return lax.ppermute(array, axis, pairs)]
    pallas_call x0 -> x1, Pallas kernels: none -> 133 us  [per_device(): pl.pallas_call(functools.partial(kernel, layer, layers, rows), out_shape=...]
    dynamic_update_slice x16 -> x0, local copies, waits for them, and re-layouts: 129 us -> none  [window_part(): window = lax.map(one_head, (heads_q, heads_k, heads_v))]
    dot_general x35 -> x0, matrix products: 101 us -> none  [the longest x16 48.8 us: one_head(): jnp.einsum('qd,kd->qk', head_q, head_k, preferred_element_type=jnp.float32)]
    unnamed x33 -> x1, local copies, waits for them, and re-layouts: 33.3 us -> 3.16 us
    add x44 -> x0, other arithmetic: 18 us -> none  [the longest x12 17.9 us: add_states(): return earlier + later]
    reduce_sum x17 -> x0, other arithmetic: 16.9 us -> none  [the longest x16 13.5 us: one_head(): weights = weights / jnp.sum(weights, axis=-1, keepdims=True)]
    ppermute x8 -> x0, starting transfers between devices: 15.4 us -> none  [from_behind(): return lax.ppermute(array, axis, pairs)]
  transfers between devices with their start and end apart: 9 -> 0, of which waited for: 6 -> 0; matrix products, arithmetic and copies ran while one was open for 36% -> 0% of each run, Pallas kernels for 0% -> 0%
where the time goes in v1:
time: 138 us; the launch traced here: 136 us
  Pallas kernels  133 us (96%)
  local copies, waits for them, and re-layouts  3.16 us (2%)
    pallas_call x1, Pallas kernels, per_device(): pl.pallas_call(functools.partial(kernel, layer, layers, rows), out_shape=...  133 us
    unnamed x1, local copies, waits for them, and re-layouts  3.16 us

profile of v1, /device:TPU:24, one launch (start us, length us, event | category | flops | bytes accessed | tf_op | source)
XLA Modules:
  0.0 136.4 jit_solution(14975362142209302788)
XLA Ops:
  0.0 133.2 %shard_map.37 = bf16[512,2048]{1,0:T(8,128)(2,1)} custom-call(bf16[512,2048]{1,0:T(8,128)(2,1)} %q_hbm.1, bf16[512,2048]{1,0:T(8,128)(2,1)} %k_hbm.1, bf16[512,2048]{1,0:T(8,128)(2,1)} %v_hbm.1), custom_call_target="tpu_custom_call" | custom-call | tf_op jit(solution)/shard_map/pallas_call | solution.py:295
  133.3 3.2 %copy.5 = bf16[512,2048]{1,0:T(8,128)(2,1)} copy(bf16[512,2048]{1,0:T(8,128)(2,1)} %shard_map.37) | data formatting | bytes 4194304

commit v2 on v1

--- a/solution.py
+++ b/solution.py
@@ -15,6 +15,8 @@
 EPSILON = 1e-06
 EXP_SCALE = math.log2(math.e) / math.sqrt(DH)
 NEG = -1e30
+SERVED = 1
+LAG = 2
 F32 = jnp.float32
 BF16 = jnp.bfloat16
 MESH = pl.DeviceIdType.MESH
@@ -47,20 +49,32 @@
     layer, layers, rows,
     q_hbm, k_hbm, v_hbm, out_hbm,
     qb, kb, vb, kh, vh, ob, o_acc, m_acc, l_acc, lin_acc, total, state_in, state_out,
+    q_back, o_serve, o_back, w_serve, w_back,
     own_sem, a_send, a_recv, z_send, z_recv, s_send, s_recv, o_own, o_send, o_recv,
+    b_send, b_recv, f_send, f_recv,
 ):
     me = lax.axis_index("seq")
     place = lax.rem(me, layer)
     level = me // layer
     base = level * layer
     heads = H // layer
+    served = min(SERVED, heads - 1)
     span = layer * rows
     tiles = span // TILE
     has_before = level > 0
     has_after = level < layers - 1
 
+    pairs = layer // 2
+    core, pair = lax.rem(place, 2), place // 2
+
+    def toward(d):
+        return lax.rem(pair + d // 2, pairs) * 2 + lax.rem(core + d % 2, 2)
+
+    def origin(d):
+        return lax.rem(pair + pairs - d // 2, pairs) * 2 + lax.rem(core + 2 - d % 2, 2)
+
     def peer(d):
-        return base + lax.rem(place + d, layer)
+        return base + toward(d)
 
     barrier = pltpu.get_barrier_semaphore()
     for d in range(1, layer):
@@ -92,7 +106,7 @@
 
     def peer_copy(c, d, t):
         return pltpu.make_async_remote_copy(
-            src_ref=sources[t].at[:, columns(lax.rem(place + d, layer), c)],
+            src_ref=sources[t].at[:, columns(toward(d), c)],
             dst_ref=targets[t].at[c, my_rows, :],
             send_sem=a_send.at[c, d - 1, t],
             recv_sem=a_recv.at[c, d - 1, t],
@@ -100,12 +114,37 @@
             device_id_type=MESH,
         )
 
-    def next_copy(c, t):
-        return pltpu.make_async_remote_copy(
-            src_ref=(kb, vb)[t].at[c],
-            dst_ref=(kh, vh)[t].at[c],
-            send_sem=z_send.at[c, t],
-            recv_sem=z_recv.at[c, t],
+    def next_copy(c, d, t):
+        if d == 0:
+            from_rows, source = my_rows, sources[t].at[:, columns(place, c)]
+        else:
+            from_rows = pl.ds(pl.multiple_of(origin(d) * rows, rows), rows)
+            source = targets[t].at[c, from_rows, :]
+        return pltpu.make_async_remote_copy(
+            src_ref=source,
+            dst_ref=(kh, vh)[t].at[c, from_rows, :],
+            send_sem=z_send.at[c, d, t],
+            recv_sem=z_recv.at[c, d, t],
+            device_id={"seq": me + layer},
+            device_id_type=MESH,
+        )
+
+    def back_copy(c):
+        return pltpu.make_async_remote_copy(
+            src_ref=qb.at[c],
+            dst_ref=q_back.at[c],
+            send_sem=b_send.at[c],
+            recv_sem=b_recv.at[c],
+            device_id={"seq": me - layer},
+            device_id_type=MESH,
+        )
+
+    def served_copy(c, t):
+        return pltpu.make_async_remote_copy(
+            src_ref=(o_serve, w_serve)[t].at[c],
+            dst_ref=(o_back, w_back)[t].at[c],
+            send_sem=f_send.at[c, t],
+            recv_sem=f_recv.at[c, t],
             device_id={"seq": me + layer},
             device_id_type=MESH,
         )
@@ -121,7 +160,7 @@
         )
 
     def out_copy(c, d):
-        to_rows = pl.ds(pl.multiple_of(lax.rem(place + d, layer) * rows, rows), rows)
+        to_rows = pl.ds(pl.multiple_of(toward(d) * rows, rows), rows)
         return pltpu.make_async_remote_copy(
             src_ref=ob.at[c, to_rows, :],
             dst_ref=out_hbm.at[:, columns(place, c)],
@@ -136,16 +175,46 @@
             ob.at[c, my_rows, :], out_hbm.at[:, columns(place, c)], o_own.at[c]
         )
 
-    def start_chunk(c):
+    def send_near(c):
         for t in range(3):
-            for d in range(layer - 1, 0, -1):
+            peer_copy(c, 1, t).start()
+            own_copy(c, t).start()
+
+    def send_far(c):
+        for t in range(3):
+            for d in range(2, layer):
                 peer_copy(c, d, t).start()
-            own_copy(c, t).start()
-
-    def wait_tensor(c, t):
-        own_copy(c, t).wait()
+
+    def wait_near(c):
+        for t in range(2):
+            peer_copy(c, 1, t).wait_recv()
+
+    def pass_near(c):
+        wait_near(c)
+
+        @pl.when(has_after)
+        def _():
+            for d in range(2):
+                for t in range(2):
+                    next_copy(c, d, t).start()
+
+    def wait_far(c):
+        for t in range(2):
+            for d in range(2, layer):
+                peer_copy(c, d, t).wait_recv()
+
+    def pass_far(c):
+        @pl.when(has_after)
+        def _():
+            for d in range(2, layer):
+                for t in range(2):
+                    next_copy(c, d, t).start()
+
+    def wait_rest(c):
+        for t in range(3):
+            own_copy(c, t).wait()
         for d in range(1, layer):
-            peer_copy(c, d, t).wait_recv()
+            peer_copy(c, d, 2).wait_recv()
 
     row_id = lax.broadcasted_iota(jnp.int32, (TILE, TILE), 0)
     col_id = lax.broadcasted_iota(jnp.int32, (TILE, TILE), 1)
@@ -184,17 +253,20 @@
             l_acc[slot, here, :] = jnp.broadcast_to(mass, (TILE, DH))
         total[c] = state
 
+    def halo_tile(i, queries, keys, values, c):
+        here = slice(i * TILE, (i + 1) * TILE)
+        q, k, v = queries[c, here, :], keys[c, here, :], values[c, here, :]
+        scores = jnp.where(col_id > row_id, dot_nt(q, k), NEG)
+        k_full = keys[c, (i + 1) * TILE :, :] if i < tiles - 1 else None
+        v_full = values[c, (i + 1) * TILE :, :] if i < tiles - 1 else None
+        return part_softmax(q, k_full, v_full, scores, v)
+
     def halo_part(c, slot):
-        inside = col_id > row_id
         state = state_in[c]
         for i in range(tiles):
             here = slice(i * TILE, (i + 1) * TILE)
-            q, k, v = qb[c, here, :], kh[c, here, :], vh[c, here, :]
-            scores = jnp.where(inside, dot_nt(q, k), NEG)
-            lin_acc[slot, here, :] += times_state(q, state)
-            k_full = kh[c, (i + 1) * TILE :, :] if i < tiles - 1 else None
-            v_full = vh[c, (i + 1) * TILE :, :] if i < tiles - 1 else None
-            peak, mass, acc = part_softmax(q, k_full, v_full, scores, v)
+            lin_acc[slot, here, :] += times_state(qb[c, here, :], state)
+            peak, mass, acc = halo_tile(i, qb, kh, vh, c)
             before = m_acc[slot, here, :]
             both = jnp.maximum(before, peak)
             keep = jnp.exp2((before - both) * EXP_SCALE)
@@ -202,54 +274,112 @@
             o_acc[slot, here, :] = o_acc[slot, here, :] * keep + acc * take
             l_acc[slot, here, :] = l_acc[slot, here, :] * keep + mass * take
 
-    start_chunk(0)
-    if heads > 1:
-        start_chunk(1)
+    def serve(c):
+        for i in range(tiles):
+            here = slice(i * TILE, (i + 1) * TILE)
+            peak, mass, acc = halo_tile(i, q_back, kb, vb, c)
+            o_serve[c, here, :] = (acc / mass).astype(BF16)
+            weight = jnp.broadcast_to(peak * EXP_SCALE + jnp.log2(mass), (TILE, DH))
+            w_serve[c, :, here] = weight.T[:8, :]
+
+    def merge_served(c, slot):
+        state = state_in[c]
+        for i in range(tiles):
+            here = slice(i * TILE, (i + 1) * TILE)
+            lin_acc[slot, here, :] += times_state(qb[c, here, :], state)
+            weight = jnp.broadcast_to(w_back[c, 0:1, here], (DH, TILE)).T
+            before = m_acc[slot, here, :] * EXP_SCALE
+            both = jnp.maximum(before, weight)
+            keep = jnp.exp2(before - both)
+            take = jnp.exp2(weight - both)
+            mean = o_back[c, here, :].astype(F32)
+            o_acc[slot, here, :] = o_acc[slot, here, :] * keep + mean * take
+            l_acc[slot, here, :] = l_acc[slot, here, :] * keep + take
+
+    send_near(0)
+    send_far(0)
+    for c in range(1, heads):
+        send_near(c)
+    pass_near(served)
 
     def step(c, _):
         @pl.when(c < heads)
         def _():
-            wait_tensor(c, 0)
-            wait_tensor(c, 1)
+            @pl.when(c < served)
+            def _():
+                wait_near(c)
+
+            wait_far(c)
+
+            @pl.when(c >= served)
+            def _():
+                pass_far(c)
+
+            @pl.when(c + 1 < heads)
+            def _():
+                send_far(c + 1)
+
+            @pl.when(c + 1 + served < heads)
+            def _():
+                pass_near(c + 1 + served)
+
+            wait_rest(c)
+
+            @pl.when(c < served)
+            def _():
+                @pl.when(has_before)
+                def _():
+                    back_copy(c).start()
+
+            local_part(c, c)
+
+        @pl.when(c > 0)
+        def _():
+            @pl.when(c <= served)
+            def _():
+                @pl.when(has_after)
+                def _():
+                    back_copy(c - 1).wait_recv()
+                    serve(c - 1)
+                    served_copy(c - 1, 0).start()
+                    served_copy(c - 1, 1).start()
+
+        @pl.when(c >= LAG)
+        def _():
+            h = c - LAG
+            slot = h
+
+            @pl.when(has_before)
+            def _():
+                state_copy(h).wait_recv()
 
             @pl.when(has_after)
             def _():
-                next_copy(c, 0).start()
-                next_copy(c, 1).start()
-
-            @pl.when(c + 2 < heads)
-            def _():
-                start_chunk(c + 2)
-
-            wait_tensor(c, 2)
-            local_part(c, lax.rem(c, 2))
-
-        @pl.when(c > 0)
-        def _():
-            h = c - 1
-            slot = lax.rem(h, 2)
+                @pl.when(has_before)
+                def _():
+                    state_out[h] = state_in[h] + total[h]
+
+                @pl.when(level == 0)
+                def _():
+                    state_out[h] = total[h]
+
+                state_copy(h).start()
 
             @pl.when(has_before)
             def _():
-                state_copy(h).wait_recv()
-
-            @pl.when(has_after)
-            def _():
-                @pl.when(has_before)
-                def _():
-                    state_out[h] = state_in[h] + total[h]
-
-                @pl.when(level == 0)
-                def _():
-                    state_out[h] = total[h]
-
-                state_copy(h).start()
-
-            @pl.when(has_before)
-            def _():
-                next_copy(h, 0).wait_recv()
-                next_copy(h, 1).wait_recv()
-                halo_part(h, slot)
+                @pl.when(h < served)
+                def _():
+                    served_copy(h, 0).wait_recv()
+                    served_copy(h, 1).wait_recv()
+                    merge_served(h, slot)
+
+                @pl.when(h >= served)
+                def _():
+                    for d in range(layer):
+                        for t in range(2):
+                            next_copy(h, d, t).wait_recv()
+
+                    halo_part(h, slot)
 
             def finish(i, _):
                 here = pl.ds(pl.multiple_of(i * TILE, TILE), TILE)
@@ -264,7 +394,7 @@
 
         return 0
 
-    lax.fori_loop(0, heads + 1, step, 0)
+    lax.fori_loop(0, heads + LAG, step, 0)
 
     def drain(c, _):
         for d in range(1, layer):
@@ -276,9 +406,24 @@
 
         @pl.when(has_after)
         def _():
-            next_copy(c, 0).wait_send()
-            next_copy(c, 1).wait_send()
+            @pl.when(c >= served)
+            def _():
+                for d in range(layer):
+                    for t in range(2):
+                        next_copy(c, d, t).wait_send()
+
+            @pl.when(c < served)
+            def _():
+                served_copy(c, 0).wait_send()
+                served_copy(c, 1).wait_send()
+
             state_copy(c).wait_send()
+
+        @pl.when(has_before)
+        def _():
+            @pl.when(c < served)
+            def _():
+                back_copy(c).wait_send()
 
         return 0
 
@@ -298,19 +443,25 @@
         in_specs=[pl.BlockSpec(memory_space=pl.ANY)] * 3,
         out_specs=pl.BlockSpec(memory_space=pl.ANY),
         scratch_shapes=[pltpu.VMEM((heads, span, DH), BF16)] * 6
-        + [pltpu.VMEM((2, span, DH), F32)] * 4
+        + [pltpu.VMEM((heads, span, DH), F32)] * 4
         + [pltpu.VMEM((heads, DH, DH), F32)] * 3
+        + [pltpu.VMEM((heads, span, DH), BF16)] * 3
+        + [pltpu.VMEM((heads, 8, span), F32)] * 2
         + [
             dma((heads, 3)),
             dma((heads, layer - 1, 3)),
             dma((heads, layer - 1, 3)),
-            dma((heads, 2)),
-            dma((heads, 2)),
+            dma((heads, layer, 2)),
+            dma((heads, layer, 2)),
             dma((heads,)),
             dma((heads,)),
             dma((heads,)),
             dma((heads, layer - 1)),
             dma((heads, layer - 1)),
+            dma((heads,)),
+            dma((heads,)),
+            dma((heads, 2)),
+            dma((heads, 2)),
         ],
         compiler_params=pltpu.CompilerParams(
             collective_id=0, has_side_effects=True, vmem_limit_bytes=56 * 2**20

time: 138 us -> 129 us (0.935)
  Pallas kernels: 133 us -> 125 us
    pallas_call x1, Pallas kernels: 133 us -> 125 us  [per_device(): pl.pallas_call(functools.partial(kernel, layer, layers, rows), out_shape=...]
where the time goes in v2:
time: 129 us; the launch traced here: 128 us
  Pallas kernels  125 us (97%)
  local copies, waits for them, and re-layouts  3.16 us (2%)
    pallas_call x1, Pallas kernels, per_device(): pl.pallas_call(functools.partial(kernel, layer, layers, rows), out_shape=...  125 us
    unnamed x1, local copies, waits for them, and re-layouts  3.16 us

profile of v2, /device:TPU:24, one launch (start us, length us, event | category | flops | bytes accessed | tf_op | source)
XLA Modules:
  0.0 128.0 jit_solution(17783359984040413339)
XLA Ops:
  0.0 124.9 %shard_map.37 = bf16[512,2048]{1,0:T(8,128)(2,1)} custom-call(bf16[512,2048]{1,0:T(8,128)(2,1)} %q_hbm.1, bf16[512,2048]{1,0:T(8,128)(2,1)} %k_hbm.1, bf16[512,2048]{1,0:T(8,128)(2,1)} %v_hbm.1), custom_call_target="tpu_custom_call" | custom-call | tf_op jit(solution)/shard_map/pallas_call | solution.py:440
  124.9 3.2 %copy.5 = bf16[512,2048]{1,0:T(8,128)(2,1)} copy(bf16[512,2048]{1,0:T(8,128)(2,1)} %shard_map.37) | data formatting | bytes 4194304

commit v3 on v2

--- a/solution.py
+++ b/solution.py
@@ -261,6 +261,19 @@
         v_full = values[c, (i + 1) * TILE :, :] if i < tiles - 1 else None
         return part_softmax(q, k_full, v_full, scores, v)
 
+    def finish(c, slot, r):
+        here = slice(r * rows, (r + 1) * rows)
+        win = o_acc[slot, here, :] / l_acc[slot, here, :]
+        ob[c, here, :] = (head_norm(lin_acc[slot, here, :]) + head_norm(win)).astype(BF16)
+        for d in range(1, layer):
+            @pl.when(toward(d) == r)
+            def _():
+                out_copy(c, d).start()
+
+        @pl.when(place == r)
+        def _():
+            out_own(c).start()
+
     def halo_part(c, slot):
         state = state_in[c]
         for i in range(tiles):
@@ -273,6 +286,8 @@
             take = jnp.exp2((peak - both) * EXP_SCALE)
             o_acc[slot, here, :] = o_acc[slot, here, :] * keep + acc * take
             l_acc[slot, here, :] = l_acc[slot, here, :] * keep + mass * take
+            if (i + 1) * TILE % rows == 0:
+                finish(c, slot, i // (rows // TILE))
 
     def serve(c):
         for i in range(tiles):
@@ -295,6 +310,8 @@
             mean = o_back[c, here, :].astype(F32)
             o_acc[slot, here, :] = o_acc[slot, here, :] * keep + mean * take
             l_acc[slot, here, :] = l_acc[slot, here, :] * keep + take
+            if (i + 1) * TILE % rows == 0:
+                finish(c, slot, i // (rows // TILE))
 
     send_near(0)
     send_far(0)
@@ -381,16 +398,10 @@
 
                     halo_part(h, slot)
 
-            def finish(i, _):
-                here = pl.ds(pl.multiple_of(i * TILE, TILE), TILE)
-                win = o_acc[slot, here, :] / l_acc[slot, here, :]
-                ob[h, here, :] = (head_norm(lin_acc[slot, here, :]) + head_norm(win)).astype(BF16)
-                return 0
-
-            lax.fori_loop(0, tiles, finish, 0)
-            for d in range(1, layer):
-                out_copy(h, d).start()
-            out_own(h).start()
+            @pl.when(level == 0)
+            def _():
+                for r in range(layer):
+                    finish(h, slot, r)
 
         return 0
 

time: 129 us -> 128 us (level)
  Pallas kernels: 125 us -> 123 us
    pallas_call x1, Pallas kernels: 125 us -> 123 us  [per_device(): pl.pallas_call(functools.partial(kernel, layer, layers, rows), out_shape=...]
where the time goes in v3:
time: 128 us; the launch traced here: 127 us
  Pallas kernels  123 us (96%)
  local copies, waits for them, and re-layouts  3.16 us (2%)
    pallas_call x1, Pallas kernels, per_device(): pl.pallas_call(functools.partial(kernel, layer, layers, rows), out_shape=...  123 us
    unnamed x1, local copies, waits for them, and re-layouts  3.16 us

profile of v3, /device:TPU:24, one launch (start us, length us, event | category | flops | bytes accessed | tf_op | source)
XLA Modules:
  0.0 126.5 jit_solution(8783854930387066614)
XLA Ops:
  0.0 123.4 %shard_map.37 = bf16[512,2048]{1,0:T(8,128)(2,1)} custom-call(bf16[512,2048]{1,0:T(8,128)(2,1)} %q_hbm.1, bf16[512,2048]{1,0:T(8,128)(2,1)} %k_hbm.1, bf16[512,2048]{1,0:T(8,128)(2,1)} %v_hbm.1), custom_call_target="tpu_custom_call" | custom-call | tf_op jit(solution)/shard_map/pallas_call | solution.py:451
  123.4 3.2 %copy.5 = bf16[512,2048]{1,0:T(8,128)(2,1)} copy(bf16[512,2048]{1,0:T(8,128)(2,1)} %shard_map.37) | data formatting | bytes 4194304
